TPU v7x, 128 devices: a whole 4x4x4 slice. The times are simulated.
128 devices in a mesh: row: 8 (over y, core), col: 16 (over z, x).
Axes of the slice: x: 4, y: 4, z: 4, core: 2. Of those that a mesh axis runs over, the one named last changes fastest.
Arguments:
- ancestor_inverse: float32 [12288, 12288], P('row', 'col')
- factor: bfloat16 [3, 12288, 512], P(None, ('row', 'col')), may hold values from -0.5 to 0.5
- coupling: float32 [3, 512, 512], replicated, may hold values from -0.25 to 0.25
- diagonal_inverse: float32 [3, 512, 512], replicated, may hold values from -6 to 6
- ancestors: int32 [3, 24], replicated, may hold values from -1 to 23, as said below
Outputs:
- block_columns: float32 [3, 12288, 512], P(None, ('row', 'col'))
- block_rows: float32 [3, 12288, 512], P(None, ('col', 'row'))
- node_blocks: float32 [3, 3, 512, 512], replicated
Inputs may be any that keep to these rules, and one draw needn't show every extreme that they name: `ancestors`: row k lists the ancestor block rows of supernode k, blocks of 512 rows: distinct indices in increasing order, then -1 in the slots left. Every block is listed by some supernode.
All inputs are finite; a program needn't handle non-finite values.
Results may differ from a plain program's by a relative error of at most 0.0003.
Values may be sent and summed in bfloat16 or wider, within the bound.
A program may use at most 128 MiB of HBM per device.

v0:
```python
import jax
import jax.numpy as jnp
from jax import lax
from jax.sharding import PartitionSpec as P

highest = lax.Precision.HIGHEST


def broadcast(value, axis, source):
    kept = jnp.where(lax.axis_index(axis) == source, value, 0).astype(value.dtype)
    return lax.psum(kept, axis)


def matmul(left, right):
    return jnp.dot(left, right, precision=highest)


def left_dot(left, right):
    return lax.dot_general(left, right, (((0,), (0,)), ((), ())), precision=highest)


def pair_index(later, earlier):
    return later * (later - 1) // 2 + earlier


def local(ancestor_inverse, factor, coupling, diagonal_inverse, ancestors):
    col_count = lax.axis_size("col")
    row_count = lax.axis_size("row")
    row_index = lax.axis_index("row")
    col_index = lax.axis_index("col")
    nodes_total, piece_rows, sn_width = factor.shape
    rows_here, cols_here = ancestor_inverse.shape
    group_ratio = rows_here // cols_here
    first_row = (row_index * col_count + col_index) * piece_rows
    block_of_row = (first_row + jnp.arange(piece_rows, dtype=jnp.int32)) // sn_width
    source_row = col_index // group_ratio
    block_start = col_index % group_ratio * cols_here
    row_layout = []
    solved = {}
    for current in range(nodes_total):
        listed = jnp.any(ancestors[current][:, None] == block_of_row[None, :], axis=0)
        lower_part = jnp.where(listed[:, None], factor[current], jnp.zeros_like(factor[current]))
        lower_rows = lax.all_gather(lower_part, "col", axis=0, tiled=True)
        own_block = lax.dynamic_slice_in_dim(lower_rows, block_start, cols_here, 0)
        lower_cols = broadcast(own_block, "row", source_row).astype(jnp.float32)
        lower_here = lower_part.astype(jnp.float32)
        product_sum = lax.psum_scatter(
            matmul(ancestor_inverse, lower_cols), "col", scatter_dimension=0, tiled=True
        )
        for earlier in range(current):
            product_sum = product_sum + matmul(
                row_layout[earlier], coupling[pair_index(current, earlier)]
            )
        column = -product_sum
        stacked = jnp.concatenate(row_layout + [column], axis=1)
        summed = lax.psum(left_dot(lower_here, stacked), ("row", "col"))
        crosses = [
            summed[:, earlier * sn_width : (earlier + 1) * sn_width] for earlier in range(current)
        ]
        self_term = summed[:, current * sn_width : (current + 1) * sn_width]
        for earlier in range(current):
            block_value = -crosses[earlier].T
            for inner in range(current):
                block_value = block_value - matmul(
                    solved[earlier, inner], coupling[pair_index(current, inner)]
                )
            solved[earlier, current] = block_value
            solved[current, earlier] = block_value.T
        diag_value = diagonal_inverse[current] - self_term
        for earlier in range(current):
            diag_value = diag_value - left_dot(
                coupling[pair_index(current, earlier)], solved[earlier, current]
            )
        solved[current, current] = diag_value
        row_layout.append(column)
    finished = jnp.stack(row_layout)
    part_rows = piece_rows // row_count
    ratio_cols = col_count // row_count
    split_parts = finished.reshape(nodes_total, row_count, part_rows, sn_width)
    held = lax.all_to_all(split_parts, "row", split_axis=1, concat_axis=1, tiled=True)
    targets = jnp.arange(row_count, dtype=jnp.int32) * ratio_cols + col_index // row_count
    onehot = (targets[:, None] == jnp.arange(col_count, dtype=jnp.int32)[None, :]).astype(
        jnp.float32
    )
    slotted = jnp.einsum("rc,nrqs->ncqs", onehot, held, precision=highest)
    arrived = lax.all_to_all(slotted, "col", split_axis=1, concat_axis=1, tiled=True)
    picked = lax.dynamic_slice_in_dim(arrived, col_index % ratio_cols * row_count, row_count, 1)
    landed = lax.all_to_all(picked, "row", split_axis=1, concat_axis=1, tiled=True)
    mirrored_all = landed.reshape(nodes_total, piece_rows, sn_width)
    node_blocks = jnp.stack(
        [
            jnp.stack([solved[first_node, second_node] for second_node in range(nodes_total)])
            for first_node in range(nodes_total)
        ]
    )
    return (finished, mirrored_all, node_blocks)


def solution(mesh):
    placed = (P("row", "col"), P(None, ("row", "col"), None), P(), P(), P())
    return jax.shard_map(
        local,
        mesh=mesh,
        in_specs=placed,
        out_specs=(P(None, ("row", "col"), None), P(None, ("col", "row"), None), P()),
        check_vma=False,
    )
```

profile of v0, /device:TPU:1, one launch (start us, length us, event | category | flops | bytes accessed | tf_op | source)
XLA Modules:
  0.0 691.0 jit_solution(10552824575240240170)
XLA Ops:
  11.5 45.6 %all-gather.6.cloned.1.call-done = bf16[1536,512]{1,0:T(8,128)(2,1)} async-done(((bf16[96,512]{1,0:T(8,128)(2,1)}), bf16[1536,512]{1,0:T(8,128)(2,1)}) %all-gather.6.cloned.1.call-update) | async-done | bytes 1572880 | tf_op jit(solution)/shard_map/all_gather | solution.py:43
  59.2 43.3 %all-gather.4.cloned.1.call-done = bf16[1536,512]{1,0:T(8,128)(2,1)} async-done(((bf16[96,512]{1,0:T(8,128)(2,1)}), bf16[1536,512]{1,0:T(8,128)(2,1)}) %all-gather.4.cloned.1.call-update) | async-done | bytes 1572880 | tf_op jit(solution)/shard_map/all_gather | solution.py:43
  104.7 43.3 %all-gather.8.cloned.1.call-done = bf16[1536,512]{1,0:T(8,128)(2,1)} async-done(((bf16[96,512]{1,0:T(8,128)(2,1)}), bf16[1536,512]{1,0:T(8,128)(2,1)}) %all-gather.8.cloned.1.call-update) | async-done | bytes 1572880 | tf_op jit(solution)/shard_map/all_gather | solution.py:43
  150.3 66.0 %all-reduce.7.cloned.1.call-done = (bf16[768,512]{1,0:T(8,128)(2,1)}, bf16[768,512]{1,0:T(8,128)(2,1)}, bf16[768,512]{1,0:T(8,128)(2,1)}) async-done(((bf16[768,512]{1,0:T(8,128)(2,1)}, bf16[768,512]{1,0:T(8,128)(2,1)}, bf16[768,512]{1,0:T(8,128)(2,1)}), (bf16[768,512]{1,0:T(8,128)(2,1)}, bf16[768,512]{1,0:T(8,128)(2,1)}, bf16[768,512]{1,0:T(8,128)(2,1)})) %all-reduce.7.cloned.1.call-update) | async-done | bytes 2359312 | tf_op jit(solution)/shard_map/psum | solution.py:11
  216.2 6.7 convolution_bitcast_fusion.2
  225.3 6.7 convolution_bitcast_fusion.1
  234.5 6.7 convolution_bitcast_fusion
  244.1 57.1 %reduce-scatter.10.cloned.1.call-done = f32[96,512]{1,0:T(8,128)} async-done(((f32[1536,512]{1,0:T(8,128)}), f32[96,512]{1,0:T(8,128)}) %reduce-scatter.10.cloned.1.call-update) | async-done | bytes 196624 | tf_op jit(solution)/shard_map/reduce_scatter | solution.py:47
  301.2 78.3 %reduce-scatter.12.cloned.1.call-done = f32[96,512]{1,0:T(8,128)} async-done(((f32[1536,512]{1,0:T(8,128)}), f32[96,512]{1,0:T(8,128)}) %reduce-scatter.12.cloned.1.call-update) | async-done | bytes 196624 | tf_op jit(solution)/shard_map/reduce_scatter | solution.py:47
  381.3 77.3 %reduce-scatter.14.cloned.1.call-done = f32[96,512]{1,0:T(8,128)} async-done(((f32[1536,512]{1,0:T(8,128)}), f32[96,512]{1,0:T(8,128)}) %reduce-scatter.14.cloned.1.call-update) | async-done | bytes 196624 | tf_op jit(solution)/shard_map/reduce_scatter | solution.py:47
  464.2 3.1 fusion.38
  475.2 6.7 all-to-all-start
  481.9 15.6 %all-to-all-done = f32[3,8,12,512]{3,2,0,1:T(8,128)} async-done(((f32[3,8,12,512]{3,2,0,1:T(8,128)}), f32[3,8,12,512]{3,2,0,1:T(8,128)}, u32[]{:S(2)}, u32[]{:S(2)}) %all-to-all-start) | async-done | bytes 589856 | tf_op jit(solution)/shard_map/all_to_all | solution.py:80
  501.5 4.8 all-to-all-start.1
  506.3 21.0 %all-to-all-done.1 = f32[3,16,12,512]{3,2,0,1:T(8,128)} async-done(((f32[3,16,12,512]{3,2,0,1:T(8,128)}), f32[3,16,12,512]{3,2,0,1:T(8,128)}, u32[]{:S(2)}, u32[]{:S(2)}) %all-to-all-start.1) | async-done | bytes 1179680 | tf_op jit(solution)/shard_map/all_to_all | solution.py:86
  529.4 9.0 %all-to-all-start.2 = ((f32[3,8,12,512]{3,2,0,1:T(8,128)}), f32[3,8,12,512]{3,2,0,1:T(8,128)}, u32[]{:S(2)}, u32[]{:S(2)}) async-start(f32[3,8,12,512]{3,2,0,1:T(8,128)} %constant_dynamic-slice_fusion), calls=%async_computation.2 | async-start | bytes 1572864 | tf_op jit(solution)/shard_map/all_to_all | solution.py:88
  545.1 5.7 all-to-all-done.2
  555.1 83.9 %all-reduce.5.cloned.1.call-done = (f32[512,1536]{1,0:T(8,128)}, f32[512,512]{1,0:T(8,128)}, f32[512,1024]{0,1:T(8,128)}) async-done(((f32[512,1536]{1,0:T(8,128)}, f32[512,512]{1,0:T(8,128)}, f32[512,1024]{0,1:T(8,128)}), (f32[512,1536]{1,0:T(8,128)}, f32[512,512]{1,0:T(8,128)}, f32[512,1024]{0,1:T(8,128)})) %all-reduce.5.cloned.1.call-update) | async-done | bytes 6291472 | tf_op jit(solution)/shard_map/psum | solution.py:56
  638.9 3.8 bitcast_subtract_fusion.7
  653.7 3.1 fusion.2
  663.9 3.8 maximum_bitcast_fusion.1
  667.8 3.6 copy.95
  671.3 4.3 fusion.1
  679.1 4.9 pad_maximum_fusion
  (102 shorter events, 72.2 us)
Async XLA Ops:
  7.2 49.9 %all-gather.6.cloned.1.call-start = ((), (), s32[]{:S(2)}) async-start(), calls=%async_computation.7 | async-start | bytes 1671168 | tf_op jit(solution)/shard_map/all_gather | solution.py:43
  9.9 92.6 %all-gather.4.cloned.1.call-start = ((), (), s32[]{:S(2)}) async-start(), calls=%async_computation.6 | async-start | bytes 1671168 | tf_op jit(solution)/shard_map/all_gather | solution.py:43
  10.7 137.4 %all-gather.8.cloned.1.call-start = ((), (), s32[]{:S(2)}) async-start(), calls=%async_computation.8 | async-start | bytes 1671168 | tf_op jit(solution)/shard_map/all_gather | solution.py:43
  11.4 204.8 %all-reduce.7.cloned.1.call-start = ((), (), s32[]{:S(2)}) async-start(), calls=%async_computation.13 | async-start | bytes 4718592 | tf_op jit(solution)/shard_map/psum | solution.py:11
  150.2 151.0 %reduce-scatter.10.cloned.1.call-start = ((), (), s32[]{:S(2)}) async-start(), calls=%async_computation.9 | async-start | bytes 3342336 | tf_op jit(solution)/shard_map/reduce_scatter | solution.py:47
  225.3 154.3 %reduce-scatter.12.cloned.1.call-start = ((), (), s32[]{:S(2)}) async-start(), calls=%async_computation.10 | async-start | bytes 3342336 | tf_op jit(solution)/shard_map/reduce_scatter | solution.py:47
  234.4 224.1 %reduce-scatter.14.cloned.1.call-start = ((), (), s32[]{:S(2)}) async-start(), calls=%async_computation.11 | async-start | bytes 3342336 | tf_op jit(solution)/shard_map/reduce_scatter | solution.py:47
  243.6 136.0 %copy-start = (f32[3,512,512]{2,1,0:T(8,128)S(1)}, f32[3,512,512]{2,1,0:T(8,128)}, u32[]{:S(2)}) copy-start(f32[3,512,512]{2,1,0:T(8,128)} %param.7) | copy-start | bytes 9437188
  243.6 395.3 %all-reduce.5.cloned.1.call-start = ((), (), s32[]{:S(2)}) async-start(), calls=%async_computation.12 | async-start | bytes 12582912 | tf_op jit(solution)/shard_map/psum | solution.py:56
  301.2 159.9 %copy-start.16 = (f32[96,512]{1,0:T(8,128)S(1)}, f32[96,512]{1,0:T(8,128)}, u32[]{:S(2)}) copy-start(f32[96,512]{1,0:T(8,128)} %reduce-scatter.10.cloned.1.call-done) | copy-start | bytes 589828
  458.6 5.7 copy-start.22
  461.1 6.2 copy-start.17
  461.9 5.5 copy-start.19
  461.9 5.5 copy-start.21
  475.2 22.3 %all-to-all-start = ((f32[3,8,12,512]{3,2,0,1:T(8,128)}), f32[3,8,12,512]{3,2,0,1:T(8,128)}, u32[]{:S(2)}, u32[]{:S(2)}) async-start(f32[3,8,12,512]{3,2,0,1:T(8,128)} %copy.78), calls=%async_computation | async-start | bytes 1572864 | tf_op jit(solution)/shard_map/all_to_all | solution.py:80
  501.5 25.8 %all-to-all-start.1 = ((f32[3,16,12,512]{3,2,0,1:T(8,128)}), f32[3,16,12,512]{3,2,0,1:T(8,128)}, u32[]{:S(2)}, u32[]{:S(2)}) async-start(f32[3,16,12,512]{3,2,0,1:T(8,128)} %copy.80), calls=%async_computation.1 | async-start | bytes 3145728 | tf_op jit(solution)/shard_map/all_to_all | solution.py:86
  529.4 21.4 %all-to-all-start.2 = ((f32[3,8,12,512]{3,2,0,1:T(8,128)}), f32[3,8,12,512]{3,2,0,1:T(8,128)}, u32[]{:S(2)}, u32[]{:S(2)}) async-start(f32[3,8,12,512]{3,2,0,1:T(8,128)} %constant_dynamic-slice_fusion), calls=%async_computation.2 | async-start | bytes 1572864 | tf_op jit(solution)/shard_map/all_to_all | solution.py:88
  642.7 5.8 copy-start.1
  646.6 12.5 %copy-start.3 = (f32[512,512]{0,1:T(8,128)}, f32[512,512]{0,1:T(8,128)S(1)}, u32[]{:S(2)}) copy-start(f32[512,512]{0,1:T(8,128)S(1)} %fusion.18) | copy-start | bytes 3145732
  648.5 5.1 copy-start.6
  653.7 5.4 copy-start.4
  671.3 4.3 copy-start.2
  671.3 4.3 copy-start.12
  671.3 4.3 copy-start.15
  (10 other events, 25.4 us)
Sparse Core Ops, SparseCore 0:
  10.7 46.3 all-gather.5
  59.2 43.3 all-gather.3
  104.7 43.3 all-gather.7
  151.0 65.1 all-reduce.6
  225.4 75.7 reduce-scatter.9
  304.4 75.1 reduce-scatter.11
  383.4 75.0 reduce-scatter.13
  469.1 169.7 all-reduce.4
where the time goes:
time: 699 us; the launch traced here: 691 us
  waiting for transfers between devices  539 us (77%)
  matrix products  54.5 us (8%)
  local copies, waits for them, and re-layouts  36 us (5%)
  other arithmetic  26 us (4%)
  starting transfers between devices  21.2 us (3%)
  between operations  14.7 us (2%)
    reduce_scatter x3, waiting for transfers between devices, local(): lax.psum_scatter(matmul(ancestor_inverse, lower_cols), 'col', scatter_dim...  213 us
    all_gather x3, waiting for transfers between devices, local(): lower_rows = lax.all_gather(lower_part, 'col', axis=0, tiled=True)  132 us
    psum x1, waiting for transfers between devices, local(): summed = lax.psum(left_dot(lower_here, stacked), ('row', 'col'))  83.9 us
    psum x1, waiting for transfers between devices, broadcast(): return lax.psum(kept, axis)  66 us
    dot_general x11, matrix products, matmul(): return jnp.dot(left, right, precision=highest)  36 us
    all_to_all x1, waiting for transfers between devices, local(): lax.all_to_all(slotted, 'col', split_axis=1, concat_axis=1, tiled=True)  21 us
    dot_general x6, matrix products, left_dot(): lax.dot_general(left, right, (((0,), (0,)), ((), ())), precision=highest)  16.5 us
    all_to_all x1, waiting for transfers between devices, local(): lax.all_to_all(split_parts, 'row', split_axis=1, concat_axis=1, tiled=True)  15.6 us
  transfers between devices with their start and end apart: 11, of which 11 were waited for; matrix products, arithmetic and copies ran while one was open for 7% of the time, Pallas kernels for 0%

commit v1 on v0

--- a/solution.py
+++ b/solution.py
@@ -4,6 +4,28 @@
 from jax.sharding import PartitionSpec as P
 
 highest = lax.Precision.HIGHEST
+
+
+def cut_along(value, dim, peers):
+    before, after = (value.shape[:dim], value.shape[dim + 1 :])
+    return jnp.moveaxis(value.reshape(*before, peers, -1, *after), dim, 0)
+
+
+def laid_out(blocks, dim):
+    blocks = jnp.moveaxis(blocks, 0, dim)
+    shape = blocks.shape
+    return blocks.reshape(*shape[:dim], shape[dim] * shape[dim + 1], *shape[dim + 2 :])
+
+
+def rotated_exchange(x, axis, split_dim, concat_dim):
+    count, place = (lax.axis_size(axis), lax.axis_index(axis))
+    blocks = cut_along(x, split_dim, count)
+    done = [blocks[place]]
+    for turn in range(1, count):
+        sent = blocks[(place + turn) % count]
+        done.append(lax.ppermute(sent, axis, [(i, (i + turn) % count) for i in range(count)]))
+    blocks = jnp.stack(done)[(place - jnp.arange(count)) % count]
+    return laid_out(blocks, concat_dim)
 
 
 def broadcast(value, axis, source):
@@ -85,7 +107,7 @@
     slotted = jnp.einsum("rc,nrqs->ncqs", onehot, held, precision=highest)
     arrived = lax.all_to_all(slotted, "col", split_axis=1, concat_axis=1, tiled=True)
     picked = lax.dynamic_slice_in_dim(arrived, col_index % ratio_cols * row_count, row_count, 1)
-    landed = lax.all_to_all(picked, "row", split_axis=1, concat_axis=1, tiled=True)
+    landed = rotated_exchange(picked, "row", 1, 1)
     mirrored_all = landed.reshape(nodes_total, piece_rows, sn_width)
     node_blocks = jnp.stack(
         [

time: 699 us -> 700 us (level)
  waiting for transfers between devices: 539 us -> 525 us
  local copies, waits for them, and re-layouts: 36 us -> 46.9 us
    ppermute x0 -> x7, starting transfers between devices: none -> 11.9 us  [rotated_exchange(): lax.ppermute(sent, axis, [(i, (i + turn) % count) for i in range(count)])]
    all_to_all x1 -> x0, starting transfers between devices: 9.01 us -> none  [local(): lax.all_to_all(picked, 'row', split_axis=1, concat_axis=1, tiled=True)]
    another operation x0 -> x3, local copies, waits for them, and re-layouts: none -> 7.49 us  [the longest x2 5.48 us: rotated_exchange(): blocks = jnp.stack(done)[(place - jnp.arange(count)) % count]]
    unnamed x50 -> x71, local copies, waits for them, and re-layouts: 14.4 us -> 18 us
  transfers between devices with their start and end apart: 11 -> 17, of which waited for: 11 -> 11; matrix products, arithmetic and copies ran while one was open for 7% -> 8% of each run, Pallas kernels for 0% -> 0%
where the time goes in v1:
time: 700 us; the launch traced here: 692 us
  waiting for transfers between devices  525 us (75%)
  matrix products  54.5 us (8%)
  local copies, waits for them, and re-layouts  46.9 us (7%)
  other arithmetic  26 us (4%)
  starting transfers between devices  24.2 us (3%)
  between operations  15 us (2%)
    reduce_scatter x3, waiting for transfers between devices, local(): lax.psum_scatter(matmul(ancestor_inverse, lower_cols), 'col', scatter_dim...  213 us
    all_gather x3, waiting for transfers between devices, local(): lower_rows = lax.all_gather(lower_part, 'col', axis=0, tiled=True)  132 us
    psum x1, waiting for transfers between devices, local(): summed = lax.psum(left_dot(lower_here, stacked), ('row', 'col'))  80.8 us
    psum x1, waiting for transfers between devices, broadcast(): return lax.psum(kept, axis)  66 us
    dot_general x11, matrix products, matmul(): return jnp.dot(left, right, precision=highest)  36 us
    unnamed x71, local copies, waits for them, and re-layouts  18 us
    dot_general x6, matrix products, left_dot(): lax.dot_general(left, right, (((0,), (0,)), ((), ())), precision=highest)  16.4 us
    all_to_all x1, waiting for transfers between devices, local(): lax.all_to_all(slotted, 'col', split_axis=1, concat_axis=1, tiled=True)  16 us
  transfers between devices with their start and end apart: 17, of which 11 were waited for; matrix products, arithmetic and copies ran while one was open for 8% of the time, Pallas kernels for 0%

profile of v1, /device:TPU:1, one launch (start us, length us, event | category | flops | bytes accessed | tf_op | source)
XLA Modules:
  0.0 691.7 jit_solution(15029344123010885238)
XLA Ops:
  11.5 45.6 %all-gather.6.cloned.1.call-done = bf16[1536,512]{1,0:T(8,128)(2,1)} async-done(((bf16[96,512]{1,0:T(8,128)(2,1)}), bf16[1536,512]{1,0:T(8,128)(2,1)}) %all-gather.6.cloned.1.call-update) | async-done | bytes 1572880 | tf_op jit(solution)/shard_map/all_gather | solution.py:65
  59.2 43.3 %all-gather.4.cloned.1.call-done = bf16[1536,512]{1,0:T(8,128)(2,1)} async-done(((bf16[96,512]{1,0:T(8,128)(2,1)}), bf16[1536,512]{1,0:T(8,128)(2,1)}) %all-gather.4.cloned.1.call-update) | async-done | bytes 1572880 | tf_op jit(solution)/shard_map/all_gather | solution.py:65
  104.7 43.3 %all-gather.8.cloned.1.call-done = bf16[1536,512]{1,0:T(8,128)(2,1)} async-done(((bf16[96,512]{1,0:T(8,128)(2,1)}), bf16[1536,512]{1,0:T(8,128)(2,1)}) %all-gather.8.cloned.1.call-update) | async-done | bytes 1572880 | tf_op jit(solution)/shard_map/all_gather | solution.py:65
  150.3 66.0 %all-reduce.7.cloned.1.call-done = (bf16[768,512]{1,0:T(8,128)(2,1)}, bf16[768,512]{1,0:T(8,128)(2,1)}, bf16[768,512]{1,0:T(8,128)(2,1)}) async-done(((bf16[768,512]{1,0:T(8,128)(2,1)}, bf16[768,512]{1,0:T(8,128)(2,1)}, bf16[768,512]{1,0:T(8,128)(2,1)}), (bf16[768,512]{1,0:T(8,128)(2,1)}, bf16[768,512]{1,0:T(8,128)(2,1)}, bf16[768,512]{1,0:T(8,128)(2,1)})) %all-reduce.7.cloned.1.call-update) | async-done | bytes 2359312 | tf_op jit(solution)/shard_map/psum | solution.py:33
  216.2 6.7 convolution_bitcast_fusion.2
  225.3 6.7 convolution_bitcast_fusion.1
  234.5 6.7 convolution_bitcast_fusion
  244.1 57.1 %reduce-scatter.10.cloned.1.call-done = f32[96,512]{1,0:T(8,128)} async-done(((f32[1536,512]{1,0:T(8,128)}), f32[96,512]{1,0:T(8,128)}) %reduce-scatter.10.cloned.1.call-update) | async-done | bytes 196624 | tf_op jit(solution)/shard_map/reduce_scatter | solution.py:69
  301.2 78.3 %reduce-scatter.12.cloned.1.call-done = f32[96,512]{1,0:T(8,128)} async-done(((f32[1536,512]{1,0:T(8,128)}), f32[96,512]{1,0:T(8,128)}) %reduce-scatter.12.cloned.1.call-update) | async-done | bytes 196624 | tf_op jit(solution)/shard_map/reduce_scatter | solution.py:69
  381.3 77.1 %reduce-scatter.14.cloned.1.call-done = f32[96,512]{1,0:T(8,128)} async-done(((f32[1536,512]{1,0:T(8,128)}), f32[96,512]{1,0:T(8,128)}) %reduce-scatter.14.cloned.1.call-update) | async-done | bytes 196624 | tf_op jit(solution)/shard_map/reduce_scatter | solution.py:69
  464.1 3.1 fusion.38
  475.1 6.7 all-to-all-start
  481.8 15.5 %all-to-all-done = f32[3,8,12,512]{3,2,0,1:T(8,128)} async-done(((f32[3,8,12,512]{3,2,0,1:T(8,128)}), f32[3,8,12,512]{3,2,0,1:T(8,128)}, u32[]{:S(2)}, u32[]{:S(2)}) %all-to-all-start) | async-done | bytes 589856 | tf_op jit(solution)/shard_map/all_to_all | solution.py:102
  501.3 4.9 all-to-all-start.1
  511.1 16.0 %all-to-all-done.1 = f32[3,16,12,512]{3,2,0,1:T(8,128)} async-done(((f32[3,16,12,512]{3,2,0,1:T(8,128)}), f32[3,16,12,512]{3,2,0,1:T(8,128)}, u32[]{:S(2)}, u32[]{:S(2)}) %all-to-all-start.1) | async-done | bytes 1179680 | tf_op jit(solution)/shard_map/all_to_all | solution.py:108
  528.5 5.0 collective-permute-start
  546.5 3.1 stack.107
  558.8 80.8 %all-reduce.5.cloned.1.call-done = (f32[512,1536]{1,0:T(8,128)}, f32[512,512]{1,0:T(8,128)}, f32[512,1024]{0,1:T(8,128)}) async-done(((f32[512,1536]{1,0:T(8,128)}, f32[512,512]{1,0:T(8,128)}, f32[512,1024]{0,1:T(8,128)}), (f32[512,1536]{1,0:T(8,128)}, f32[512,512]{1,0:T(8,128)}, f32[512,1024]{0,1:T(8,128)})) %all-reduce.5.cloned.1.call-update) | async-done | bytes 6291472 | tf_op jit(solution)/shard_map/psum | solution.py:78
  639.6 3.8 bitcast_subtract_fusion.7
  654.3 3.0 fusion.2
  664.6 3.8 maximum_bitcast_fusion.1
  668.4 3.5 copy.168
  672.0 4.3 fusion.1
  679.7 4.9 pad_maximum_fusion
  (141 shorter events, 87.4 us)
Async XLA Ops:
  7.2 49.9 %all-gather.6.cloned.1.call-start = ((), (), s32[]{:S(2)}) async-start(), calls=%async_computation.6 | async-start | bytes 1671168 | tf_op jit(solution)/shard_map/all_gather | solution.py:65
  9.9 92.6 %all-gather.4.cloned.1.call-start = ((), (), s32[]{:S(2)}) async-start(), calls=%async_computation.5 | async-start | bytes 1671168 | tf_op jit(solution)/shard_map/all_gather | solution.py:65
  10.7 137.3 %all-gather.8.cloned.1.call-start = ((), (), s32[]{:S(2)}) async-start(), calls=%async_computation.7 | async-start | bytes 1671168 | tf_op jit(solution)/shard_map/all_gather | solution.py:65
  11.4 204.8 %all-reduce.7.cloned.1.call-start = ((), (), s32[]{:S(2)}) async-start(), calls=%async_computation.12 | async-start | bytes 4718592 | tf_op jit(solution)/shard_map/psum | solution.py:33
  150.2 151.0 %reduce-scatter.10.cloned.1.call-start = ((), (), s32[]{:S(2)}) async-start(), calls=%async_computation.8 | async-start | bytes 3342336 | tf_op jit(solution)/shard_map/reduce_scatter | solution.py:69
  225.3 154.3 %reduce-scatter.12.cloned.1.call-start = ((), (), s32[]{:S(2)}) async-start(), calls=%async_computation.9 | async-start | bytes 3342336 | tf_op jit(solution)/shard_map/reduce_scatter | solution.py:69
  234.4 224.0 %reduce-scatter.14.cloned.1.call-start = ((), (), s32[]{:S(2)}) async-start(), calls=%async_computation.10 | async-start | bytes 3342336 | tf_op jit(solution)/shard_map/reduce_scatter | solution.py:69
  243.5 136.0 %copy-start = (f32[3,512,512]{2,1,0:T(8,128)S(1)}, f32[3,512,512]{2,1,0:T(8,128)}, u32[]{:S(2)}) copy-start(f32[3,512,512]{2,1,0:T(8,128)} %param.7) | copy-start | bytes 9437188
  243.6 396.0 %all-reduce.5.cloned.1.call-start = ((), (), s32[]{:S(2)}) async-start(), calls=%async_computation.11 | async-start | bytes 12582912 | tf_op jit(solution)/shard_map/psum | solution.py:78
  301.2 159.8 %copy-start.16 = (f32[96,512]{1,0:T(8,128)S(1)}, f32[96,512]{1,0:T(8,128)}, u32[]{:S(2)}) copy-start(f32[96,512]{1,0:T(8,128)} %reduce-scatter.10.cloned.1.call-done) | copy-start | bytes 589828
  458.4 5.7 copy-start.22
  461.0 6.2 copy-start.17
  461.7 5.5 copy-start.19
  475.1 22.2 %all-to-all-start = ((f32[3,8,12,512]{3,2,0,1:T(8,128)}), f32[3,8,12,512]{3,2,0,1:T(8,128)}, u32[]{:S(2)}, u32[]{:S(2)}) async-start(f32[3,8,12,512]{3,2,0,1:T(8,128)} %copy.143), calls=%async_computation | async-start | bytes 1572864 | tf_op jit(solution)/shard_map/all_to_all | solution.py:102
  501.3 25.8 %all-to-all-start.1 = ((f32[3,16,12,512]{3,2,0,1:T(8,128)}), f32[3,16,12,512]{3,2,0,1:T(8,128)}, u32[]{:S(2)}, u32[]{:S(2)}) async-start(f32[3,16,12,512]{3,2,0,1:T(8,128)} %copy.145), calls=%async_computation.1 | async-start | bytes 3145728 | tf_op jit(solution)/shard_map/all_to_all | solution.py:108
  528.5 12.0 %collective-permute-start = (f32[3,1,12,512]{3,1,2,0:T(1,128)S(1)}, f32[3,1,12,512]{3,1,2,0:T(1,128)S(1)}, u32[]{:S(2)}, u32[]{:S(2)}) collective-permute-start(f32[3,1,12,512]{3,1,2,0:T(1,128)S(1)} %copy.183), channel_id=1, source_target_pairs={{0,16},{16,32},{32,48},{48,64},{64,80},{80,96},{96,112},{112,0},{1... | collective-permute-start | bytes 221192 | tf_op jit(solution)/shard_map/ppermute | solution.py:26
  533.6 7.0 %collective-permute-start.1 = (f32[3,1,12,512]{3,1,2,0:T(1,128)S(1)}, f32[3,1,12,512]{3,1,2,0:T(1,128)S(1)}, u32[]{:S(2)}, u32[]{:S(2)}) collective-permute-start(f32[3,1,12,512]{3,1,2,0:T(1,128)S(1)} %copy.184), channel_id=1, source_target_pairs={{0,32},{16,48},{32,64},{48,80},{64,96},{80,112},{96,0},{112,16},{1... | collective-permute-start | bytes 221192 | tf_op jit(solution)/shard_map/ppermute | solution.py:26
  533.8 9.5 %collective-permute-start.2 = (f32[3,1,12,512]{3,1,2,0:T(1,128)S(1)}, f32[3,1,12,512]{3,1,2,0:T(1,128)S(1)}, u32[]{:S(2)}, u32[]{:S(2)}) collective-permute-start(f32[3,1,12,512]{3,1,2,0:T(1,128)S(1)} %copy.185), channel_id=1, source_target_pairs={{0,48},{16,64},{32,80},{48,96},{64,112},{80,0},{96,16},{112,32},{1... | collective-permute-start | bytes 221192 | tf_op jit(solution)/shard_map/ppermute | solution.py:26
  535.2 8.2 %collective-permute-start.3 = (f32[3,1,12,512]{3,1,2,0:T(1,128)S(1)}, f32[3,1,12,512]{3,1,2,0:T(1,128)S(1)}, u32[]{:S(2)}, u32[]{:S(2)}) collective-permute-start(f32[3,1,12,512]{3,1,2,0:T(1,128)S(1)} %copy.186), channel_id=1, source_target_pairs={{0,64},{16,80},{32,96},{48,112},{64,0},{80,16},{96,32},{112,48},{1... | collective-permute-start | bytes 221192 | tf_op jit(solution)/shard_map/ppermute | solution.py:26
  537.6 6.3 collective-permute-start.4
  540.5 4.1 collective-permute-start.5
  540.6 4.6 collective-permute-start.6
  643.4 5.8 copy-start.1
  647.2 12.5 %copy-start.3 = (f32[512,512]{0,1:T(8,128)}, f32[512,512]{0,1:T(8,128)S(1)}, u32[]{:S(2)}) copy-start(f32[512,512]{0,1:T(8,128)S(1)} %fusion.18) | copy-start | bytes 3145732
  (23 other events, 62.6 us)
Sparse Core Ops, SparseCore 0:
  10.7 46.3 all-gather.5
  59.2 43.3 all-gather.3
  104.7 43.3 all-gather.7
  151.0 65.1 all-reduce.6
  225.4 75.7 reduce-scatter.9
  304.4 75.0 reduce-scatter.11
  383.4 74.9 reduce-scatter.13
  469.0 170.5 all-reduce.4
